TPU v7x, 256 devices: a whole 4x4x8 slice. The times are simulated.
256 devices in a mesh: group: 32 (over x, y, core), mp: 8 (over z).
Axes of the slice: x: 4, y: 4, z: 8, core: 2. Of those that a mesh axis runs over, the one named last changes fastest.
Arguments:
- hidden: bfloat16 [16384, 1792], P('group')
- norm_gain: float32 [1792], replicated, may hold values from 0.1 to 1.9
- qkv_weight: bfloat16 [1792, 2304], P(None, 'mp'), may hold values from -0.125 to 0.125
- out_weight: bfloat16 [1792, 1792], P('mp'), may hold values from -0.125 to 0.125
- adapter_down: bfloat16 [1792, 1024], P(None, 'mp'), may hold values from -0.125 to 0.125
- adapter_up: bfloat16 [1024, 1792], P('mp'), may hold values from -1.5 to 1.5
- vocab_rows: bfloat16 [4096, 1792], P(('group', 'mp')), may hold values from -0.125 to 0.125
- segments: int32 [16384], P('group'), may hold values from 0 to 127, never falling along the last dimension, each value on 1 to 512 neighbouring positions
- request_adapter: int32 [128], replicated, may hold values from 0 to 63
- adapter_slot: int32 [64], replicated, may hold values from 0 to 63, each once
- page_table: int32 [2048], replicated, may hold values from 0 to 2047, as said below
Outputs:
- layer_update: bfloat16 [16384, 1792], P('group', 'mp')
- state_norms: float32 [16, 16384], P('mp', 'group')
- max_logits: float32 [16384], P(('group', 'mp'))
Inputs may be any that keep to these rules, and one draw needn't show every extreme that they name: A permutation of all pages. Logical page k of group g (entry g * 64 + k) lies in group page_table[g * 64 + k] // 64, and every group holds exactly two of the logical pages of every group. `segments`: every request's tokens stand together and in order; no request has more than 512 tokens. `adapter_slot`: A permutation.
All inputs are finite; a program needn't handle non-finite values.
Results may differ from a plain program's by a relative error of at most 0.013.
Values may be sent and summed in bfloat16 or wider, within the bound.
A program may use at most 64 MiB of HBM per device.

v0:
```python
import jax
import jax.numpy as jnp
from jax import lax
from jax.sharding import PartitionSpec as P

FEAT = 16
HD = 112
RANK = 16
EPSILON = 1e-05
PRECISE = lax.Precision.HIGHEST


def from_behind(value, axis, by):
    size = lax.axis_size(axis)
    pairs = [(i, i + by) for i in range(size) if 0 <= i + by < size]
    return lax.ppermute(value, axis, pairs)


def rms_normed(values, norm_gain):
    wide = values.astype(jnp.float32)
    meansq = jnp.mean(wide * wide, axis=-1, keepdims=True)
    return (wide * lax.rsqrt(meansq + EPSILON) * norm_gain).astype(jnp.bfloat16)


def features(vectors, feat_width):
    linear_part = vectors / feat_width**0.25
    outer_part = (vectors[..., :, None] * vectors[..., None, :]).reshape(
        vectors.shape[:-1] + (feat_width * feat_width,)
    )
    outer_part = outer_part / (2.0 * feat_width) ** 0.5
    ones_part = jnp.ones(vectors.shape[:-1] + (1,), jnp.float32)
    return jnp.concatenate([ones_part, linear_part, outer_part], axis=-1)


def block_step(state_carry, block_inputs, feat_width):
    states, totals, owner_seg = state_carry
    phi_query, phi_key, query_rows, key_rows, value_rows, seg_ids = block_inputs
    scaling = feat_width ** (-0.5)
    block_len = seg_ids.shape[0]
    position = jnp.arange(block_len, dtype=jnp.int32)
    allowed = (
        (position[:, None] >= position[None, :]) & (seg_ids[:, None] == seg_ids[None, :])
    ).astype(jnp.float32)
    carried = (seg_ids == owner_seg).astype(jnp.float32)[None, :]
    scores = jnp.einsum("hcf,hdf->hcd", query_rows, key_rows, precision=PRECISE) * scaling
    weights = (1.0 + scores + 0.5 * scores * scores) * allowed[None]
    numerator = jnp.einsum("hcd,hde->hce", weights, value_rows, precision=PRECISE)
    numerator = numerator + carried[..., None] * jnp.einsum(
        "hcp,hpe->hce", phi_query, states, precision=PRECISE
    )
    denominator = jnp.sum(weights, axis=-1) + carried * jnp.einsum(
        "hcp,hp->hc", phi_query, totals, precision=PRECISE
    )
    mixed_out = numerator / denominator[..., None]
    key_scores = jnp.einsum("hcf,hdf->hcd", key_rows, key_rows, precision=PRECISE) * scaling
    value_gram = jnp.einsum("hce,hde->hcd", value_rows, value_rows, precision=PRECISE)
    key_gram = (1.0 + key_scores + 0.5 * key_scores * key_scores) * value_gram
    masked_gram = jnp.einsum("cd,hde->hce", allowed, key_gram, precision=PRECISE)
    local_squares = jnp.sum(masked_gram * allowed[None], axis=-1)
    along = jnp.sum(
        jnp.einsum("hcp,hpe->hce", phi_key, states, precision=PRECISE) * value_rows, axis=-1
    )
    cross_squares = jnp.einsum("cd,hd->hc", allowed, along, precision=PRECISE)
    state_squares = jnp.sum(states * states, axis=(1, 2))
    squares = carried * (state_squares[:, None] + 2.0 * cross_squares) + local_squares
    counted = carried * totals[:, :1] + jnp.sum(allowed, axis=-1)[None, :]
    state_norm = jnp.sqrt(squares / (counted * (feat_width * value_rows.shape[-1])))
    last_seg = seg_ids[-1]
    member = (seg_ids == last_seg).astype(jnp.float32)
    continues = (owner_seg == last_seg).astype(jnp.float32)
    new_states = continues * states + jnp.einsum(
        "hcp,hce->hpe", phi_key * member[None, :, None], value_rows, precision=PRECISE
    )
    new_totals = continues * totals + jnp.einsum("hcp,c->hp", phi_key, member, precision=PRECISE)
    return ((new_states, new_totals, last_seg), (mixed_out, state_norm))


def best_of(candidates, piece):
    logits = jnp.einsum("rd,vd->rv", candidates, piece, preferred_element_type=jnp.float32)
    return jnp.max(logits, axis=1)


def on_device(
    hidden,
    norm_gain,
    qkv_weight,
    out_weight,
    adapter_down,
    adapter_up,
    vocab_rows,
    segments,
    request_adapter,
    adapter_slot,
    page_table,
):
    groups = lax.axis_size("group")
    own_group = lax.axis_index("group")
    shards = lax.axis_size("mp")
    own_shard = lax.axis_index("mp")
    rows_here = segments.shape[0]
    model_width = hidden.shape[1]
    slice_width = model_width // shards
    table = page_table.reshape(groups, -1)
    per_group = table.shape[1]
    per_peer = per_group // groups
    page_len = rows_here // per_group
    holders = table // per_group
    position = jnp.arange(per_group, dtype=jnp.int32)
    sort_keys = jnp.where(holders == own_group, position[None, :], per_group + position[None, :])
    ranked = jnp.argsort(sort_keys, axis=1)[:, :per_peer]
    picked = jnp.take_along_axis(table, ranked, axis=1) - own_group * per_group
    outgoing = hidden.reshape(per_group, page_len, model_width)[picked]
    normed_pages = rms_normed(outgoing, norm_gain)
    projected_pages = jnp.einsum(
        "abrd,dc->abrc", normed_pages, qkv_weight, preferred_element_type=jnp.float32
    ).astype(jnp.bfloat16)
    lowered_pages = jnp.einsum(
        "abrd,dc->abrc", normed_pages, adapter_down, preferred_element_type=jnp.float32
    ).astype(jnp.bfloat16)
    kept_pages = lax.dynamic_slice_in_dim(outgoing, own_shard * slice_width, slice_width, 3)
    arrived = (
        lax.all_to_all(kept_pages, "group", split_axis=0, concat_axis=0, tiled=True),
        lax.all_to_all(projected_pages, "group", split_axis=0, concat_axis=0, tiled=True),
        lax.all_to_all(lowered_pages, "group", split_axis=0, concat_axis=0, tiled=True),
    )
    own_holders = lax.dynamic_index_in_dim(holders, own_group, 0, keepdims=False)
    onehot = (own_holders[:, None] == jnp.arange(groups, dtype=jnp.int32)[None, :]).astype(
        jnp.int32
    )
    earlier = jnp.sum((jnp.cumsum(onehot, axis=0) - onehot) * onehot, axis=1)
    source_rows = own_holders * per_peer + earlier

    def placed(received):
        gathered_rows = received.reshape((groups * per_peer,) + received.shape[2:])[source_rows]
        return gathered_rows.reshape((rows_here,) + received.shape[3:])

    residual, projected, lowered = [placed(received) for received in arrived]
    heads_here = projected.shape[1] // (2 * FEAT + HD)
    split_heads = jnp.transpose(
        projected.reshape(rows_here, heads_here, 2 * FEAT + HD).astype(jnp.float32), (1, 0, 2)
    )
    query_rows = split_heads[..., :FEAT]
    key_rows = split_heads[..., FEAT : 2 * FEAT]
    value_rows = split_heads[..., 2 * FEAT :]
    phi_query = features(query_rows, FEAT)
    phi_key = features(key_rows, FEAT)
    last_seg = segments[-1]
    member = (segments == last_seg).astype(jnp.float32)
    end_state = jnp.einsum(
        "hcp,hce->hpe", phi_key * member[None, :, None], value_rows, precision=PRECISE
    )
    end_totals = jnp.einsum("hcp,c->hp", phi_key, member, precision=PRECISE)
    end_tag = jnp.reshape(last_seg + 1, (1,)).astype(jnp.float32)
    got_state, got_totals, got_tag = (
        from_behind(end_state.astype(jnp.bfloat16), "group", 1).astype(end_state.dtype),
        from_behind(end_totals.astype(jnp.bfloat16), "group", 1).astype(end_totals.dtype),
        from_behind(end_tag.astype(jnp.bfloat16), "group", 1).astype(end_tag.dtype),
    )
    initial = (got_state, got_totals, got_tag[0].astype(jnp.int32) - 1)
    block_len = min(256, rows_here)
    blocks = rows_here // block_len

    def regroup(values):
        return jnp.transpose(
            values.reshape(values.shape[0], blocks, block_len, values.shape[-1]), (1, 0, 2, 3)
        )

    scan_inputs = (
        regroup(phi_query),
        regroup(phi_key),
        regroup(query_rows),
        regroup(key_rows),
        regroup(value_rows),
        segments.reshape(blocks, block_len),
    )

    def scan_step(state_carry, block_inputs):
        return block_step(state_carry, block_inputs, FEAT)

    _, (mixed_out, state_norm) = lax.scan(scan_step, initial, scan_inputs)
    attended = (
        jnp.transpose(mixed_out, (0, 2, 1, 3))
        .reshape(rows_here, heads_here * HD)
        .astype(jnp.bfloat16)
    )
    state_norms = jnp.transpose(state_norm, (1, 0, 2)).reshape(heads_here, rows_here)
    request_ids = jnp.arange(request_adapter.shape[0], dtype=jnp.int32)
    adapter_of = jnp.sum(
        jnp.where(segments[:, None] == request_ids[None, :], request_adapter[None, :], 0), axis=1
    )
    adapter_ids = jnp.arange(adapter_slot.shape[0], dtype=jnp.int32)
    slot_ids = jnp.sum(
        jnp.where(adapter_of[:, None] == adapter_ids[None, :], adapter_slot[None, :], 0), axis=1
    )
    column_slot = jnp.arange(lowered.shape[1], dtype=jnp.int32) // RANK
    local_slot = slot_ids - own_shard * (lowered.shape[1] // RANK)
    low_rank = jnp.where(
        local_slot[:, None] == column_slot[None, :], lowered, jnp.zeros_like(lowered)
    )
    partial_value = jnp.dot(attended, out_weight, preferred_element_type=jnp.float32)
    partial_value = partial_value + jnp.dot(
        low_rank, adapter_up, preferred_element_type=jnp.float32
    )
    summed = lax.psum_scatter(
        partial_value.astype(jnp.bfloat16), "mp", scatter_dimension=1, tiled=True
    )
    final_rows = (residual.astype(jnp.float32) + summed.astype(jnp.float32)).astype(jnp.bfloat16)
    own_rows = lax.all_to_all(final_rows, "mp", split_axis=0, concat_axis=1, tiled=True)
    max_logits = best_of(own_rows, lax.all_gather(vocab_rows, ("group", "mp"), axis=0, tiled=True))
    return (summed, state_norms, max_logits)


def solution(mesh):
    placed = (
        P("group", None),
        P(),
        P(None, "mp"),
        P("mp", None),
        P(None, "mp"),
        P("mp", None),
        P(("group", "mp"), None),
        P("group"),
        P(),
        P(),
        P(),
    )
    return jax.shard_map(
        on_device,
        mesh=mesh,
        in_specs=placed,
        out_specs=(P("group", "mp"), P("mp", "group"), P(("group", "mp"))),
        check_vma=False,
    )
```

profile of v0, /device:TPU:1, one launch (start us, length us, event | category | flops | bytes accessed | tf_op | source)
XLA Modules:
  0.0 277.1 jit_solution(12786450912121898422)
XLA Ops:
  8.0 1.4 slice.34
  10.1 5.3 %collective-permute-start.2 = (bf16[1]{0:T(256)(128)(2,1)}, bf16[1]{0:T(256)(128)(2,1)}, u32[]{:S(2)}, u32[]{:S(2)}) collective-permute-start(bf16[1]{0:T(256)(128)(2,1)} %bitcast.30), channel_id=1, source_target_pairs={{0,8},{8,16},{16,24},{24,32},{32,40},{40,48},{48,56},{56,64},{64,7... | collective-permute-start | bytes 14 | tf_op jit(solution)/shard_map/ppermute | solution.py:16
  15.4 0.8 reshape.237
  16.2 1.0 sort.17
  17.5 0.8 gather_fusion.4
  18.7 1.9 gather_fusion
  20.6 2.0 fusion.49
  22.8 3.0 %fusion.59 = bf16[32,2,8,128]{3,2,1,0:T(8,128)(2,1)} fusion(bf16[32,2,8,1792]{3,2,1,0:T(8,128)(2,1)} %bitcast.226, f32[1792]{0:T(1024)S(1)} %copy-done.19, f32[32,2,8]{2,1,0:T(2,128)S(1)} %copy.95, bf16[1792,128]{1,0:T(8,128)(2,1)} %param.17), kind=kOutput, calls=%fused_computation.84 | convolution fusion | flops 238616576 | bytes 2434048 | tf_op jit(solution)/shard_map/abrd,dc->abrc/dot_general | solution.py:117
  25.8 6.9 %all-to-all-start.1 = ((bf16[32,2,8,128]{3,2,1,0:T(8,128)(2,1)}), bf16[32,2,8,128]{3,2,1,0:T(8,128)(2,1)S(1)}, u32[]{:S(2)}, u32[]{:S(2)}) async-start(bf16[32,2,8,128]{3,2,1,0:T(8,128)(2,1)} %fusion.59), calls=%async_computation.1 | async-start | bytes 262144 | tf_op jit(solution)/shard_map/all_to_all | solution.py:124
  33.4 3.4 %fusion.56 = bf16[32,2,8,288]{3,2,1,0:T(8,128)(2,1)} fusion(bf16[32,2,8,1792]{3,2,1,0:T(8,128)(2,1)} %bitcast.227, f32[1792]{0:T(1024)S(1)} %copy-done.19, f32[32,2,8]{2,1,0:T(2,128)S(1)} %copy.95, bf16[1792,288]{0,1:T(8,128)(2,1)S(1)} %copy-done.18), kind=kOutput, calls=%fused_computation.81 | convolution fusion | flops 532299776 | bytes 3171328 | tf_op jit(solution)/shard_map/abrd,dc->abrc/dot_general | solution.py:114
  38.2 2.2 all-to-all-done.1
  40.4 5.2 %all-to-all-start = ((bf16[32,2,8,288]{3,2,1,0:T(8,128)(2,1)}), bf16[32,2,8,288]{3,2,1,0:T(8,128)(2,1)S(1)}, u32[]{:S(2)}, u32[]{:S(2)}) async-start(bf16[32,2,8,288]{3,2,1,0:T(8,128)(2,1)} %fusion.56), calls=%async_computation | async-start | bytes 786432 | tf_op jit(solution)/shard_map/all_to_all | solution.py:123
  47.6 1.3 gather_fusion.2
  48.8 7.1 %all-to-all-done = bf16[32,2,8,288]{3,2,1,0:T(8,128)(2,1)S(1)} async-done(((bf16[32,2,8,288]{3,2,1,0:T(8,128)(2,1)}), bf16[32,2,8,288]{3,2,1,0:T(8,128)(2,1)S(1)}, u32[]{:S(2)}, u32[]{:S(2)}) %all-to-all-start) | async-done | bytes 294944 | tf_op jit(solution)/shard_map/all_to_all | solution.py:123
  57.3 0.8 copy-done.4
  58.4 1.3 pad_maximum_fusion.1
  59.7 1.3 convolution_convert_fusion
  61.0 1.9 collective-permute-start
  62.9 0.7 fusion.80
  63.6 0.8 copy.114
  64.4 2.6 collective-permute-start.1
  67.0 1.5 bitcast_bitcast_fusion.1
  68.5 1.7 reshape.241
  70.2 0.8 copy.135
  71.7 1.7 reshape.245
  73.4 0.9 convert_element_type.128
  74.3 0.9 convert_element_type.126
  75.2 48.3 %while.21 = (s32[]{:T(128)}, f32[2,273,112]{2,1,0:T(8,128)S(1)}, f32[2,273]{0,1:T(8,128)S(1)}, s32[]{:T(128)}, bf16[2,2,256,112]{2,3,1,0:T(8,128)(2,1)}, /*index...) while((s32[]{:T(128)}, f32[2,273,112]{2,1,0:T(8,128)S(1)}, ...), condition=%wide.region_10.11_spmd, body=%wide.region_4.10_spmd.sunk | while | flops 1377437056 | bytes 16456851 | solution.py:180
  75.9 2.5 constant_dynamic-slice_fusion.7
  78.4 1.5 fusion.142
  79.9 1.3 compare_convert_fusion.5
  81.2 1.3 dynamic-slice.2
  83.2 1.6 convolution_multiply_fusion.6
  85.4 1.7 convolution_add_fusion.3
  87.8 1.0 fusion.134
  89.0 0.8 fusion.135
  89.9 1.1 copy.152
  90.9 1.5 fusion.136
  93.0 0.7 fusion.138
  93.7 2.1 fusion.139
  96.4 0.7 convolution_multiply_fusion.7
  100.0 2.5 constant_dynamic-slice_fusion.7
  102.6 1.5 fusion.142
  104.1 1.3 compare_convert_fusion.5
  105.3 1.3 dynamic-slice.2
  107.3 1.6 convolution_multiply_fusion.6
  109.5 1.7 convolution_add_fusion.3
  111.9 1.0 fusion.134
  113.2 0.8 fusion.135
  114.0 1.1 copy.152
  115.1 1.5 fusion.136
  117.1 0.7 fusion.138
  117.8 2.1 fusion.139
  123.5 1.2 copy.102
  124.8 1.9 fusion.81
  126.7 2.0 add_convert_fusion
  129.3 1.1 constant_dynamic-slice_fusion.3
  130.5 14.5 %all_to_all.34 = bf16[32,2,8,224]{3,2,1,0:T(8,128)(2,1)S(1)} all-to-all(bf16[32,2,8,224]{3,2,1,0:T(8,128)(2,1)S(1)} %constant_dynamic-slice_fusion.3), channel_id=1, replica_groups=mesh['group'=32,'mp'=8] {'group'}, dimensions={0} | all-to-all | bytes 458752 | tf_op jit(solution)/shard_map/all_to_all | solution.py:122
  144.9 0.7 gather_fusion.3
  145.9 21.4 %reduce-scatter.2.cloned.1.call-done = bf16[512,224]{0,1:T(8,128)(2,1)} async-done(((bf16[512,1792]{0,1:T(8,128)(2,1)}), bf16[512,224]{0,1:T(8,128)(2,1)}) %reduce-scatter.2.cloned.1.call-update) | async-done | bytes 229392 | tf_op jit(solution)/shard_map/reduce_scatter | solution.py:204
  167.3 1.0 add_convert_fusion.1
  168.4 14.1 %all_to_all.35 = bf16[8,64,224]{2,1,0:T(8,128)(2,1)S(1)} all-to-all(bf16[8,64,224]{2,1,0:T(8,128)(2,1)S(1)} %bitcast.244), channel_id=1, replica_groups=mesh['group'=32,'mp'=8] {'mp'}, dimensions={0} | all-to-all | bytes 458752 | tf_op jit(solution)/shard_map/all_to_all | solution.py:208
  183.0 76.4 %all-gather.2.cloned.1.call-done = bf16[4096,1792]{1,0:T(8,128)(2,1)} async-done(((bf16[16,1792]{1,0:T(8,128)(2,1)}), bf16[4096,1792]{1,0:T(8,128)(2,1)}) %all-gather.2.cloned.1.call-update) | async-done | bytes 14680080 | tf_op jit(solution)/shard_map/all_gather | solution.py:209
  259.4 10.3 %convolution_reduce_fusion = f32[64]{0:T(128)} fusion(bf16[64,1792]{1,0:T(8,128)(2,1)S(1)} %all_to_all.29, bf16[4096,1792]{1,0:T(8,128)(2,1)} %all-gather.2.cloned.1.call-done), kind=kOutput, calls=%fused_computation.82 | convolution fusion | flops 939786176 | bytes 14909696 | tf_op jit(solution)/shard_map/rd,vd->rv/dot_general | solution.py:79
  (139 shorter events, 18.2 us)
Async XLA Ops:
  8.0 10.7 %copy-start = (bf16[512,1792]{1,0:T(8,128)(2,1)S(1)}, bf16[512,1792]{1,0:T(8,128)(2,1)}, u32[]{:S(2)}) copy-start(bf16[512,1792]{1,0:T(8,128)(2,1)} %param.13) | copy-start | bytes 5505028
  10.1 36.8 %collective-permute-start.2 = (bf16[1]{0:T(256)(128)(2,1)}, bf16[1]{0:T(256)(128)(2,1)}, u32[]{:S(2)}, u32[]{:S(2)}) collective-permute-start(bf16[1]{0:T(256)(128)(2,1)} %bitcast.30), channel_id=1, source_target_pairs={{0,8},{8,16},{16,24},{24,32},{32,40},{40,48},{48,56},{56,64},{64,7... | collective-permute-start | bytes 14 | tf_op jit(solution)/shard_map/ppermute | solution.py:16
  20.6 2.1 copy-start.19
  22.8 9.9 %copy-start.11 = (s32[512]{0:T(512)S(1)}, s32[512]{0:T(512)}, u32[]{:S(2)}) copy-start(s32[512]{0:T(512)} %param.20) | copy-start | bytes 6148
  22.8 10.6 %copy-start.18 = (bf16[1792,288]{0,1:T(8,128)(2,1)S(1)}, bf16[1792,288]{0,1:T(8,128)(2,1)}, u32[]{:S(2)}) copy-start(bf16[1792,288]{0,1:T(8,128)(2,1)} %param.15) | copy-start | bytes 3096580
  25.8 14.6 %all-to-all-start.1 = ((bf16[32,2,8,128]{3,2,1,0:T(8,128)(2,1)}), bf16[32,2,8,128]{3,2,1,0:T(8,128)(2,1)S(1)}, u32[]{:S(2)}, u32[]{:S(2)}) async-start(bf16[32,2,8,128]{3,2,1,0:T(8,128)(2,1)} %fusion.59), calls=%async_computation.1 | async-start | bytes 262144 | tf_op jit(solution)/shard_map/all_to_all | solution.py:124
  33.4 3.8 %copy-start.16 = (s32[128]{0:T(128)S(1)}, s32[128]{0:T(128)}, u32[]{:S(2)}) copy-start(s32[128]{0:T(128)} %param.21) | copy-start | bytes 1540
  33.4 4.7 %copy-start.17 = (s32[64]{0:T(128)S(1)}, s32[64]{0:T(128)}, u32[]{:S(2)}) copy-start(s32[64]{0:T(128)} %param.22) | copy-start | bytes 772
  37.5 19.8 %copy-start.14 = (s32[1024]{0:T(1024)}, s32[1024]{0:T(1024)S(1)}, u32[]{:S(2)}) copy-start(s32[1024]{0:T(1024)S(1)} %pad_clamp_fusion) | copy-start | bytes 12292
  40.4 15.5 %all-to-all-start = ((bf16[32,2,8,288]{3,2,1,0:T(8,128)(2,1)}), bf16[32,2,8,288]{3,2,1,0:T(8,128)(2,1)S(1)}, u32[]{:S(2)}, u32[]{:S(2)}) async-start(bf16[32,2,8,288]{3,2,1,0:T(8,128)(2,1)} %fusion.56), calls=%async_computation | async-start | bytes 786432 | tf_op jit(solution)/shard_map/all_to_all | solution.py:123
  45.6 121.7 %reduce-scatter.2.cloned.1.call-start = ((), (), s32[]{:S(2)}) async-start(), calls=%async_computation.5 | async-start | bytes 2064384 | tf_op jit(solution)/shard_map/reduce_scatter | solution.py:204
  57.3 0.8 copy-start.4
  57.3 2.4 copy-start.5
  61.0 13.3 %collective-permute-start = (bf16[2,273,112]{2,1,0:T(8,128)(2,1)}, bf16[2,273,112]{2,1,0:T(8,128)(2,1)}, u32[]{:S(2)}, u32[]{:S(2)}) collective-permute-start(bf16[2,273,112]{2,1,0:T(8,128)(2,1)} %convolution_convert_fusion), channel_id=1, source_target_pairs={{0,8},{8,16},{16,24},{24,32},{32,40},{40,48},{48,56},{56,64},{64,7... | collective-permute-start | bytes 366920 | tf_op jit(solution)/shard_map/ppermute | solution.py:16
  63.6 6.7 %slice-start = ((f32[2,512,144]{1,2,0:T(8,128)}), f32[2,512,112]{1,2,0:T(8,128)S(1)}, s32[]{:S(2)}) async-start(f32[2,512,144]{1,2,0:T(8,128)} %copy-done.4), calls=%async_computation.7 | async-start | bytes 917504 | tf_op jit(solution)/shard_map/slice | solution.py:144
  64.4 9.0 %collective-permute-start.1 = (bf16[2,273]{0,1:T(8,128)(2,1)}, bf16[2,273]{0,1:T(8,128)(2,1)}, u32[]{:S(2)}, u32[]{:S(2)}) collective-permute-start(bf16[2,273]{0,1:T(8,128)(2,1)} %bitcast.250), channel_id=1, source_target_pairs={{0,8},{8,16},{16,24},{24,32},{32,40},{40,48},{48,56},{56,64},{64,7... | collective-permute-start | bytes 3284 | tf_op jit(solution)/shard_map/ppermute | solution.py:16
  70.2 1.4 copy-start.3
  75.2 3.2 %copy-start.1 = (f32[2,2,256,112]{2,3,1,0:T(8,128)S(1)}, f32[2,2,256,112]{2,3,1,0:T(8,128)}, u32[]{:S(2)}) copy-start(f32[2,2,256,112]{2,3,1,0:T(8,128)} %get-tuple-element.408) | copy-start | bytes 1376260 | tf_op jit(solution)/shard_map/while
  88.8 4.8 %copy-start.2 = (f32[2,2,256,112]{2,3,1,0:T(8,128)S(1)}, f32[2,2,256,112]{2,3,1,0:T(8,128)}, u32[]{:S(2)}) copy-start(f32[2,2,256,112]{2,3,1,0:T(8,128)} %get-tuple-element.408) | copy-start | bytes 1376260 | tf_op jit(solution)/shard_map/while
  90.9 4.8 %copy-start.6 = (f32[2,2,256,16]{2,3,1,0:T(8,128)S(1)}, f32[2,2,256,16]{2,3,1,0:T(8,128)}, u32[]{:S(2)}) copy-start(f32[2,2,256,16]{2,3,1,0:T(8,128)} %get-tuple-element.410) | copy-start | bytes 196612 | tf_op jit(solution)/shard_map/while
  93.6 4.1 %copy-start.9 = (f32[1,256]{1,0:T(1,128)S(1)}, f32[1,256]{1,0:T(1,128)}, u32[]{:S(2)}) copy-start(f32[1,256]{1,0:T(1,128)} %get-tuple-element.369) | copy-start | bytes 3076 | tf_op jit(solution)/shard_map/while
  93.6 4.1 %copy-start.10 = (f32[2,256]{1,0:T(2,128)S(1)}, f32[2,256]{1,0:T(2,128)}, u32[]{:S(2)}) copy-start(f32[2,256]{1,0:T(2,128)} %fusion.142) | copy-start | bytes 6148 | tf_op jit(solution)/shard_map/while
  93.6 4.1 %copy-start.12 = (f32[2]{0:T(128)S(1)}, f32[2]{0:T(128)}, u32[]{:S(2)}) copy-start(f32[2]{0:T(128)} %multiply_reduce_fusion.2) | copy-start | bytes 28 | tf_op jit(solution)/shard_map/while
  93.7 4.1 %copy-start.20 = (f32[2,2,256]{2,1,0:T(2,128)S(1)}, f32[2,2,256]{2,1,0:T(2,128)}, u32[]{:S(2)}) copy-start(f32[2,2,256]{2,1,0:T(2,128)} %get-tuple-element.390) | copy-start | bytes 12292 | tf_op jit(solution)/shard_map/while
  93.7 4.1 %copy-start.22 = (f32[2]{0:T(128)S(1)}, f32[2]{0:T(128)}, u32[]{:S(2)}) copy-start(f32[2]{0:T(128)} %slice_bitcast_fusion.2) | copy-start | bytes 28 | tf_op jit(solution)/shard_map/while
  98.1 0.6 copy-start.21
  99.4 3.2 %copy-start.1 = (f32[2,2,256,112]{2,3,1,0:T(8,128)S(1)}, f32[2,2,256,112]{2,3,1,0:T(8,128)}, u32[]{:S(2)}) copy-start(f32[2,2,256,112]{2,3,1,0:T(8,128)} %get-tuple-element.408) | copy-start | bytes 1376260 | tf_op jit(solution)/shard_map/while
  113.0 4.8 %copy-start.2 = (f32[2,2,256,112]{2,3,1,0:T(8,128)S(1)}, f32[2,2,256,112]{2,3,1,0:T(8,128)}, u32[]{:S(2)}) copy-start(f32[2,2,256,112]{2,3,1,0:T(8,128)} %get-tuple-element.408) | copy-start | bytes 1376260 | tf_op jit(solution)/shard_map/while
  115.1 4.8 %copy-start.6 = (f32[2,2,256,16]{2,3,1,0:T(8,128)S(1)}, f32[2,2,256,16]{2,3,1,0:T(8,128)}, u32[]{:S(2)}) copy-start(f32[2,2,256,16]{2,3,1,0:T(8,128)} %get-tuple-element.410) | copy-start | bytes 196612 | tf_op jit(solution)/shard_map/while
  117.8 4.1 %copy-start.9 = (f32[1,256]{1,0:T(1,128)S(1)}, f32[1,256]{1,0:T(1,128)}, u32[]{:S(2)}) copy-start(f32[1,256]{1,0:T(1,128)} %get-tuple-element.369) | copy-start | bytes 3076 | tf_op jit(solution)/shard_map/while
  117.8 4.1 %copy-start.10 = (f32[2,256]{1,0:T(2,128)S(1)}, f32[2,256]{1,0:T(2,128)}, u32[]{:S(2)}) copy-start(f32[2,256]{1,0:T(2,128)} %fusion.142) | copy-start | bytes 6148 | tf_op jit(solution)/shard_map/while
  117.8 4.1 %copy-start.12 = (f32[2]{0:T(128)S(1)}, f32[2]{0:T(128)}, u32[]{:S(2)}) copy-start(f32[2]{0:T(128)} %multiply_reduce_fusion.2) | copy-start | bytes 28 | tf_op jit(solution)/shard_map/while
  117.8 4.1 %copy-start.20 = (f32[2,2,256]{2,1,0:T(2,128)S(1)}, f32[2,2,256]{2,1,0:T(2,128)}, u32[]{:S(2)}) copy-start(f32[2,2,256]{2,1,0:T(2,128)} %get-tuple-element.390) | copy-start | bytes 12292 | tf_op jit(solution)/shard_map/while
  117.8 4.1 %copy-start.22 = (f32[2]{0:T(128)S(1)}, f32[2]{0:T(128)}, u32[]{:S(2)}) copy-start(f32[2]{0:T(128)} %slice_bitcast_fusion.2) | copy-start | bytes 28 | tf_op jit(solution)/shard_map/while
  122.3 0.6 copy-start.21
  124.7 1.9 copy-start.7
  124.7 1.9 copy-start.8
  124.8 1.9 copy-start.13
  124.8 1.9 copy-start.15
  128.8 130.6 %all-gather.2.cloned.1.call-start = ((), (), s32[]{:S(2)}) async-start(), calls=%async_computation.6 | async-start | bytes 14737408 | tf_op jit(solution)/shard_map/all_gather | solution.py:209
Sparse Core Ops, SparseCore 0:
  128.9 38.3 reduce-scatter.1
Sparse Core Ops, SparseCore 1:
  132.8 126.5 all-gather.1
where the time goes:
time: 278 us; the launch traced here: 277 us
  waiting for transfers between devices  108 us (39%)
  matrix products  46.6 us (17%)
  local copies, waits for them, and re-layouts  33.4 us (12%)
  blocking collectives  28.6 us (10%)
  starting transfers between devices  22 us (8%)
  other arithmetic  18.6 us (7%)
  between operations  17.3 us (6%)
  loops' own time  2.95 us (1%)
    all_gather x1, waiting for transfers between devices, on_device(): lax.all_gather(vocab_rows, ('group', 'mp'), axis=0, tiled=True)  76.4 us
    reduce_scatter x1, waiting for transfers between devices, on_device(): lax.psum_scatter(partial_value.astype(jnp.bfloat16), 'mp', scatter_dimens...  21.4 us
    all_to_all x1, blocking collectives, on_device(): lax.all_to_all(kept_pages, 'group', split_axis=0, concat_axis=0, tiled=True)  14.5 us
    all_to_all x1, blocking collectives, on_device(): lax.all_to_all(final_rows, 'mp', split_axis=0, concat_axis=1, tiled=True)  14.1 us
    dot_general x1, matrix products, best_of(): jnp.einsum('rd,vd->rv', candidates, piece, preferred_element_type=jnp.flo...  10.3 us
    ppermute x3, starting transfers between devices, from_behind(): return lax.ppermute(value, axis, pairs)  9.84 us
    all_to_all x1, waiting for transfers between devices, on_device(): lax.all_to_all(projected_pages, 'group', split_axis=0, concat_axis=0, til...  7.1 us
    all_to_all x1, starting transfers between devices, on_device(): lax.all_to_all(lowered_pages, 'group', split_axis=0, concat_axis=0, tiled...  6.91 us
  transfers between devices with their start and end apart: 7, of which 4 were waited for; matrix products, arithmetic and copies ran while one was open for 11% of the time, Pallas kernels for 0%

commit v1 on v0

--- a/solution.py
+++ b/solution.py
@@ -206,7 +206,15 @@
     )
     final_rows = (residual.astype(jnp.float32) + summed.astype(jnp.float32)).astype(jnp.bfloat16)
     own_rows = lax.all_to_all(final_rows, "mp", split_axis=0, concat_axis=1, tiled=True)
-    max_logits = best_of(own_rows, lax.all_gather(vocab_rows, ("group", "mp"), axis=0, tiled=True))
+    max_logits = best_of(
+        own_rows,
+        jnp.concatenate(
+            lax.all_to_all(
+                jnp.stack([vocab_rows] * lax.axis_size(("group", "mp"))), ("group", "mp"), 0, 0
+            ),
+            axis=0,
+        ),
+    )
     return (summed, state_norms, max_logits)
 
 

time: 278 us -> 515 us (1.85)
  waiting for transfers between devices: 108 us -> 352 us
  starting transfers between devices: 22 us -> 34.9 us
  matrix products: 46.6 us -> 37.3 us
  other arithmetic: 18.6 us -> 11.2 us
    all_to_all x0 -> x1, waiting for transfers between devices: none -> 319 us  [on_device(): lax.all_to_all(jnp.stack([vocab_rows] * lax.axis_size(('group', 'mp'))),...]
    all_gather x1 -> x0, waiting for transfers between devices: 76.4 us -> none  [on_device(): lax.all_gather(vocab_rows, ('group', 'mp'), axis=0, tiled=True)]
    all_to_all x0 -> x1, starting transfers between devices: none -> 13.4 us  [on_device(): lax.all_to_all(jnp.stack([vocab_rows] * lax.axis_size(('group', 'mp'))),...]
    another operation x2 -> x3, local copies, waits for them, and re-layouts: 0.17 us -> 6.31 us  [the longest x1 6.14 us: on_device(): jnp.stack([vocab_rows] * lax.axis_size(('group', 'mp')))]
  transfers between devices with their start and end apart: 7 -> 7, of which waited for: 4 -> 4; matrix products, arithmetic and copies ran while one was open for 11% -> 5% of each run, Pallas kernels for 0% -> 0%
where the time goes in v1:
time: 515 us; the launch traced here: 513 us
  waiting for transfers between devices  352 us (68%)
  matrix products  37.3 us (7%)
  starting transfers between devices  34.9 us (7%)
  local copies, waits for them, and re-layouts  30.2 us (6%)
  blocking collectives  28.5 us (6%)
  between operations  15.8 us (3%)
  other arithmetic  11.2 us (2%)
    all_to_all x1, waiting for transfers between devices, on_device(): lax.all_to_all(jnp.stack([vocab_rows] * lax.axis_size(('group', 'mp'))),...  319 us
    reduce_scatter x1, waiting for transfers between devices, on_device(): lax.psum_scatter(partial_value.astype(jnp.bfloat16), 'mp', scatter_dimens...  22 us
    all_to_all x1, blocking collectives, on_device(): lax.all_to_all(kept_pages, 'group', split_axis=0, concat_axis=0, tiled=True)  14.5 us
    all_to_all x1, blocking collectives, on_device(): lax.all_to_all(final_rows, 'mp', split_axis=0, concat_axis=1, tiled=True)  14 us
    all_to_all x1, starting transfers between devices, on_device(): lax.all_to_all(jnp.stack([vocab_rows] * lax.axis_size(('group', 'mp'))),...  13.4 us
  transfers between devices with their start and end apart: 7, of which 4 were waited for; matrix products, arithmetic and copies ran while one was open for 5% of the time, Pallas kernels for 0%

profile of v1, /device:TPU:1, one launch (start us, length us, event | category | flops | bytes accessed | tf_op | source)
XLA Modules:
  0.0 513.0 jit_solution(10938335262686065353)
XLA Ops:
  7.2 1.4 slice.34
  9.2 5.3 %collective-permute-start.2 = (bf16[1]{0:T(256)(128)(2,1)}, bf16[1]{0:T(256)(128)(2,1)}, u32[]{:S(2)}, u32[]{:S(2)}) collective-permute-start(bf16[1]{0:T(256)(128)(2,1)} %bitcast.30), channel_id=1, source_target_pairs={{0,8},{8,16},{16,24},{24,32},{32,40},{40,48},{48,56},{56,64},{64,7... | collective-permute-start | bytes 14 | tf_op jit(solution)/shard_map/ppermute | solution.py:16
  14.5 0.8 reshape.242
  15.4 1.0 sort.17
  16.6 0.8 gather_fusion.4
  17.9 1.9 gather_fusion
  19.8 2.0 fusion.49
  22.0 3.0 fusion.59
  25.0 6.9 %all-to-all-start.1 = ((bf16[32,2,8,128]{3,2,1,0:T(8,128)(2,1)}), bf16[32,2,8,128]{3,2,1,0:T(8,128)(2,1)S(1)}, u32[]{:S(2)}, u32[]{:S(2)}) async-start(bf16[32,2,8,128]{3,2,1,0:T(8,128)(2,1)} %fusion.59), calls=%async_computation.1 | async-start | bytes 262144 | tf_op jit(solution)/shard_map/all_to_all | solution.py:124
  31.9 0.7 fusion.78
  33.2 3.4 fusion.56
  36.8 2.8 all-to-all-done.1
  39.6 4.6 all-to-all-start
  44.9 1.3 gather_fusion.2
  46.2 8.4 %all-to-all-done = bf16[32,2,8,288]{3,2,1,0:T(8,128)(2,1)S(1)} async-done(((bf16[32,2,8,288]{3,2,1,0:T(8,128)(2,1)}), bf16[32,2,8,288]{3,2,1,0:T(8,128)(2,1)S(1)}, u32[]{:S(2)}, u32[]{:S(2)}) %all-to-all-start) | async-done | bytes 294944 | tf_op jit(solution)/shard_map/all_to_all | solution.py:123
  54.5 0.6 gather_fusion.1
  55.9 0.8 copy-done.3
  57.0 1.3 pad_maximum_fusion.1
  58.2 0.7 fusion.80
  58.9 0.8 copy.114
  59.7 1.9 collective-permute-start.1
  61.6 1.3 convolution_convert_fusion
  63.0 2.8 collective-permute-start
  65.7 1.5 bitcast_bitcast_fusion.1
  67.2 1.7 reshape.246
  69.0 3.0 reshape.250
  72.0 0.9 convert_element_type.128
  72.9 0.9 convert_element_type.126
  73.9 24.3 %while.21 = (s32[]{:T(128)}, f32[2,273,112]{2,1,0:T(8,128)S(1)}, f32[2,273]{0,1:T(8,128)S(1)}, s32[]{:T(128)}, bf16[2,2,256,112]{2,3,1,0:T(8,128)(2,1)}, /*index...) while((s32[]{:T(128)}, f32[2,273,112]{2,1,0:T(8,128)S(1)}, ...), condition=%wide.region_10.11_spmd, body=%wide.region_4.10_spmd.sunk | while | flops 1377437056 | bytes 23302216 | solution.py:180
  73.9 0.6 dynamic-slice.2
  75.5 0.7 compare_convert_fusion.6
  76.5 0.6 fusion.140
  77.1 0.7 convolution_multiply_fusion.7
  77.8 0.5 fusion.141
  78.3 0.7 fusion.136
  79.1 1.2 constant_dynamic-slice_fusion.7
  80.7 0.9 convolution_multiply_fusion.6
  82.1 0.9 fusion.142
  83.3 1.0 fusion.134
  84.4 0.8 convolution_add_fusion.3
  86.0 0.6 dynamic-slice.2
  87.6 0.7 compare_convert_fusion.6
  88.6 0.6 fusion.140
  89.3 0.7 convolution_multiply_fusion.7
  89.9 0.5 fusion.141
  90.4 0.7 fusion.136
  91.2 1.2 constant_dynamic-slice_fusion.7
  92.8 0.9 convolution_multiply_fusion.6
  94.2 0.9 fusion.142
  95.4 1.0 fusion.134
  96.5 0.8 convolution_add_fusion.3
  98.1 1.2 copy.102
  99.4 1.9 fusion.81
  101.3 2.0 add_convert_fusion
  103.3 1.1 constant_dynamic-slice_fusion.3
  104.5 14.5 %all_to_all.39 = bf16[32,2,8,224]{3,2,1,0:T(8,128)(2,1)S(1)} all-to-all(bf16[32,2,8,224]{3,2,1,0:T(8,128)(2,1)S(1)} %constant_dynamic-slice_fusion.3), channel_id=1, replica_groups=mesh['group'=32,'mp'=8] {'group'}, dimensions={0} | all-to-all | bytes 458752 | tf_op jit(solution)/shard_map/all_to_all | solution.py:122
  119.0 0.6 gather_fusion.3
  119.8 22.0 %reduce-scatter.2.cloned.1.call-done = bf16[512,224]{0,1:T(8,128)(2,1)} async-done(((bf16[512,1792]{0,1:T(8,128)(2,1)}), bf16[512,224]{0,1:T(8,128)(2,1)}) %reduce-scatter.2.cloned.1.call-update) | async-done | bytes 229392 | tf_op jit(solution)/shard_map/reduce_scatter | solution.py:204
  141.8 1.0 add_convert_fusion.1
  142.9 14.0 %all_to_all.40 = bf16[8,64,224]{2,1,0:T(8,128)(2,1)S(1)} all-to-all(bf16[8,64,224]{2,1,0:T(8,128)(2,1)S(1)} %bitcast.245), channel_id=1, replica_groups=mesh['group'=32,'mp'=8] {'mp'}, dimensions={0} | all-to-all | bytes 458752 | tf_op jit(solution)/shard_map/all_to_all | solution.py:208
  156.9 6.1 %stack.2 = bf16[256,16,1792]{2,1,0:T(8,128)(2,1)} broadcast(bf16[16,1792]{1,0:T(8,128)(2,1)S(1)} %copy-done.11), dimensions={1,2} | broadcast | bytes 14737408 | tf_op jit(solution)/shard_map/stack | solution.py:213
  163.1 13.4 %all-to-all-start.4 = ((bf16[256,16,1792]{2,1,0:T(8,128)(2,1)}), bf16[256,16,1792]{2,1,0:T(8,128)(2,1)}, u32[]{:S(2)}, u32[]{:S(2)}) async-start(bf16[256,16,1792]{2,1,0:T(8,128)(2,1)} %stack.2), calls=%async_computation.5 | async-start | bytes 29360128 | tf_op jit(solution)/shard_map/all_to_all | solution.py:212
  177.0 318.9 %all-to-all-done.4 = bf16[256,16,1792]{2,1,0:T(8,128)(2,1)} async-done(((bf16[256,16,1792]{2,1,0:T(8,128)(2,1)}), bf16[256,16,1792]{2,1,0:T(8,128)(2,1)}, u32[]{:S(2)}, u32[]{:S(2)}) %all-to-all-start.4) | async-done | bytes 14680096 | tf_op jit(solution)/shard_map/all_to_all | solution.py:212
  495.8 10.3 %convolution_reduce_fusion = f32[64]{0:T(128)} fusion(bf16[64,1792]{1,0:T(8,128)(2,1)S(1)} %all_to_all.32, bf16[4096,1792]{1,0:T(8,128)(2,1)} %bitcast.49), kind=kOutput, calls=%fused_computation.82 | convolution fusion | flops 939786176 | bytes 14909696 | tf_op jit(solution)/shard_map/rd,vd->rv/dot_general | solution.py:79
  (119 shorter events, 7.8 us)
Async XLA Ops:
  7.2 10.7 %copy-start = (bf16[512,1792]{1,0:T(8,128)(2,1)S(1)}, bf16[512,1792]{1,0:T(8,128)(2,1)}, u32[]{:S(2)}) copy-start(bf16[512,1792]{1,0:T(8,128)(2,1)} %param.13) | copy-start | bytes 5505028
  9.2 35.1 %collective-permute-start.2 = (bf16[1]{0:T(256)(128)(2,1)}, bf16[1]{0:T(256)(128)(2,1)}, u32[]{:S(2)}, u32[]{:S(2)}) collective-permute-start(bf16[1]{0:T(256)(128)(2,1)} %bitcast.30), channel_id=1, source_target_pairs={{0,8},{8,16},{16,24},{24,32},{32,40},{40,48},{48,56},{56,64},{64,7... | collective-permute-start | bytes 14 | tf_op jit(solution)/shard_map/ppermute | solution.py:16
  19.8 2.1 copy-start.16
  22.0 9.9 %copy-start.12 = (s32[512]{0:T(512)S(1)}, s32[512]{0:T(512)}, u32[]{:S(2)}) copy-start(s32[512]{0:T(512)} %param.20) | copy-start | bytes 6148
  22.0 10.6 %copy-start.13 = (s32[128]{0:T(128)S(1)}, s32[128]{0:T(128)}, u32[]{:S(2)}) copy-start(s32[128]{0:T(128)} %param.21) | copy-start | bytes 1540
  22.0 11.2 %copy-start.15 = (bf16[1792,288]{0,1:T(8,128)(2,1)S(1)}, bf16[1792,288]{0,1:T(8,128)(2,1)}, u32[]{:S(2)}) copy-start(bf16[1792,288]{0,1:T(8,128)(2,1)} %param.15) | copy-start | bytes 3096580
  25.0 14.6 %all-to-all-start.1 = ((bf16[32,2,8,128]{3,2,1,0:T(8,128)(2,1)}), bf16[32,2,8,128]{3,2,1,0:T(8,128)(2,1)S(1)}, u32[]{:S(2)}, u32[]{:S(2)}) async-start(bf16[32,2,8,128]{3,2,1,0:T(8,128)(2,1)} %fusion.59), calls=%async_computation.1 | async-start | bytes 262144 | tf_op jit(solution)/shard_map/all_to_all | solution.py:124
  33.2 3.5 copy-start.14
  39.6 14.9 %all-to-all-start = ((bf16[32,2,8,288]{3,2,1,0:T(8,128)(2,1)}), bf16[32,2,8,288]{3,2,1,0:T(8,128)(2,1)S(1)}, u32[]{:S(2)}, u32[]{:S(2)}) async-start(bf16[32,2,8,288]{3,2,1,0:T(8,128)(2,1)} %fusion.56), calls=%async_computation | async-start | bytes 786432 | tf_op jit(solution)/shard_map/all_to_all | solution.py:123
  44.2 97.6 %reduce-scatter.2.cloned.1.call-start = ((), (), s32[]{:S(2)}) async-start(), calls=%async_computation.6 | async-start | bytes 2064384 | tf_op jit(solution)/shard_map/reduce_scatter | solution.py:204
  55.8 0.8 copy-start.3
  55.9 2.4 copy-start.4
  59.7 12.3 %collective-permute-start.1 = (bf16[2,273]{0,1:T(8,128)(2,1)}, bf16[2,273]{0,1:T(8,128)(2,1)}, u32[]{:S(2)}, u32[]{:S(2)}) collective-permute-start(bf16[2,273]{0,1:T(8,128)(2,1)} %bitcast.141), channel_id=1, source_target_pairs={{0,8},{8,16},{16,24},{24,32},{32,40},{40,48},{48,56},{56,64},{64,7... | collective-permute-start | bytes 3284 | tf_op jit(solution)/shard_map/ppermute | solution.py:16
  63.0 6.0 %slice-start = ((f32[2,512,144]{1,2,0:T(8,128)}), f32[2,512,112]{1,2,0:T(8,128)S(1)}, s32[]{:S(2)}) async-start(f32[2,512,144]{1,2,0:T(8,128)} %copy-done.3), calls=%async_computation.7 | async-start | bytes 917504 | tf_op jit(solution)/shard_map/slice | solution.py:144
  63.0 9.9 %collective-permute-start = (bf16[2,273,112]{2,1,0:T(8,128)(2,1)}, bf16[2,273,112]{2,1,0:T(8,128)(2,1)}, u32[]{:S(2)}, u32[]{:S(2)}) collective-permute-start(bf16[2,273,112]{2,1,0:T(8,128)(2,1)} %convolution_convert_fusion), channel_id=1, source_target_pairs={{0,8},{8,16},{16,24},{24,32},{32,40},{40,48},{48,56},{56,64},{64,7... | collective-permute-start | bytes 366920 | tf_op jit(solution)/shard_map/ppermute | solution.py:16
  68.9 4.9 copy-start.5
  69.0 4.9 copy-start.10
  76.5 2.6 copy-start.1
  76.5 2.6 copy-start.2
  79.1 2.5 copy-start.8
  82.1 3.3 copy-start.9
  88.6 2.6 copy-start.1
  88.6 2.6 copy-start.2
  91.2 2.5 copy-start.8
  94.2 3.3 copy-start.9
  98.1 3.2 copy-start.17
  99.4 1.9 copy-start.6
  99.4 1.9 copy-start.7
  119.6 37.4 %copy-start.11 = (bf16[16,1792]{1,0:T(8,128)(2,1)S(1)}, bf16[16,1792]{1,0:T(8,128)(2,1)}, u32[]{:S(2)}) copy-start(bf16[16,1792]{1,0:T(8,128)(2,1)} %param.19) | copy-start | bytes 172036
  163.1 332.8 %all-to-all-start.4 = ((bf16[256,16,1792]{2,1,0:T(8,128)(2,1)}), bf16[256,16,1792]{2,1,0:T(8,128)(2,1)}, u32[]{:S(2)}, u32[]{:S(2)}) async-start(bf16[256,16,1792]{2,1,0:T(8,128)(2,1)} %stack.2), calls=%async_computation.5 | async-start | bytes 29360128 | tf_op jit(solution)/shard_map/all_to_all | solution.py:212
Sparse Core Ops, SparseCore 0:
  103.5 38.2 reduce-scatter.1
